TPU v7x, 128 devices: a whole 4x4x4 slice. The times are simulated.
128 devices in a mesh: req: 8 (over z, core), wide: 16 (over x, y).
Axes of the slice: x: 4, y: 4, z: 4, core: 2. Of those that a mesh axis runs over, the one named last changes fastest.
Arguments:
- queries: bfloat16 [16384, 3072], P(('req', 'wide'))
- suffix_latent: bfloat16 [16384, 512], P(('req', 'wide')), may hold values from -6 to 6
- suffix_rope: bfloat16 [64, 16384], P(None, ('req', 'wide')), may hold values from -6 to 6
- residual: bfloat16 [16384, 2048], P(('req', 'wide')), may hold values from -3 to 3
- prefix_latent: bfloat16 [8, 2, 2048, 512], P('req', None, 'wide'), may hold values from -6 to 6
- prefix_rope: bfloat16 [8, 2, 64, 2048], P('req', None, None, 'wide')
- suffix_lengths: int32 [128, 4], P(('req', 'wide')), may hold values from 1 to 64, 128 in all within a row
- prefix_ids: int32 [128, 4], P(('req', 'wide')), may hold values from 0 to 1
- w_ukv: bfloat16 [512, 4096], replicated, may hold values from -0.25 to 0.25
- w_out: bfloat16 [2048, 2048], replicated, may hold values from -0.5 to 0.5
- norm_gain: bfloat16 [2048], replicated, may hold values from 0.099609375 to 1.8984375
- expert_ids: int32 [16384, 6], P(('req', 'wide')), may hold values from 0 to 63, all different within a row; in each aligned block of 128 rows (0 to 127, 128 to 255, ...) at most 13 rows name the same one
- gate_values: float32 [16384, 6], P(('req', 'wide')), may hold values from 0.05 to 0.45
- expert_gate_up: bfloat16 [128, 2048, 1408], P(('req', 'wide')), may hold values from -0.125 to 0.125
- expert_down: bfloat16 [128, 704, 2048], P(('req', 'wide')), may hold values from -0.15625 to 0.15625
Outputs:
- layer_out: bfloat16 [16384, 2048], P(('req', 'wide'))
Inputs may be any that keep to these rules, and one draw needn't show every extreme that they name: `suffix_lengths`: row b gives, in order, the lengths of the 4 requests that make up tokens b * 128 to (b + 1) * 128 - 1; each row sums to 128 and its largest entry is 64. `expert_ids`: a token's 6 experts differ; among the 128 tokens of one device no expert is named more than 13 times, and in some device one expert is named exactly 13 times.
All inputs are finite; a program needn't handle non-finite values.
Results may differ from a plain program's by a relative error of at most 0.012.
Values may be sent and summed in bfloat16 or wider, within the bound.
No kernel may reach another device: no remote copies, remote signals or barrier semaphores. Data moves between devices by JAX's collectives and lax.ppermute only.
A program may use at most 192 MiB of HBM per device.

v0:
```python
import jax
import jax.numpy as jnp
from jax import lax
from jax.sharding import PartitionSpec as P

D = 2048
HEADS = 16
NOPE = 128
ROPE = 64
LAT = 512
TOP = 6
PREF = 2
epsilon = 1e-06


def request_tables(lengths, request_ids, token_count):
    request_end = jnp.cumsum(lengths)
    positions = jnp.arange(token_count, dtype=jnp.int32)
    segment = jnp.sum((positions[:, None] >= request_end[None, :]).astype(jnp.int32), axis=1)
    matches = segment[:, None] == jnp.arange(request_ids.shape[0], dtype=jnp.int32)[None, :]
    prefix = jnp.sum(jnp.where(matches, request_ids[None, :], 0), axis=1)
    return (segment, prefix)


def split_kv(latent, w_ukv):
    row_count = latent.shape[0]
    joined = jnp.dot(latent, w_ukv, preferred_element_type=jnp.float32).astype(jnp.bfloat16)
    joined = joined.reshape(row_count, HEADS, 2 * NOPE).transpose(1, 0, 2)
    return (joined[:, :, :NOPE], joined[:, :, NOPE:])


def split_queries(query_rows):
    row_count = query_rows.shape[0]
    query_nope = query_rows[:, : HEADS * NOPE].reshape(row_count, HEADS, NOPE).transpose(1, 0, 2)
    query_rope = query_rows[:, HEADS * NOPE :].reshape(row_count, HEADS, ROPE).transpose(1, 0, 2)
    return (query_nope, query_rope)


def head_scores(head_nope, head_rope, head_keys, rope_keys):
    scaling = 1.0 / (NOPE + ROPE) ** 0.5
    content = lax.dot_general(
        head_nope, head_keys, (((1,), (1,)), ((), ())), preferred_element_type=jnp.float32
    )
    rotary = jnp.dot(head_rope, rope_keys, preferred_element_type=jnp.float32)
    return (content + rotary) * scaling


def block_partials(query_nope, query_rope, block_keys, block_values, rope_keys, allowed):

    def one_head(operands):
        head_nope, head_rope, head_keys, head_values = operands
        scores = jnp.where(
            allowed, head_scores(head_nope, head_rope, head_keys, rope_keys), -jnp.inf
        )
        maximum = jnp.max(scores, axis=1).astype(jnp.bfloat16)
        weights = jnp.where(allowed, jnp.exp(scores - maximum.astype(jnp.float32)[:, None]), 0.0)
        summed = jnp.sum(weights, axis=1).astype(jnp.bfloat16)
        weighted = jnp.dot(
            weights.astype(jnp.bfloat16), head_values, preferred_element_type=jnp.float32
        ).astype(jnp.bfloat16)
        return (weighted, maximum, summed)

    return lax.map(one_head, (query_nope, query_rope, block_keys, block_values))


def body(
    queries,
    suffix_latent,
    suffix_rope,
    residual,
    prefix_latent,
    prefix_rope,
    suffix_lengths,
    prefix_ids,
    w_ukv,
    w_out,
    norm_gain,
    expert_ids,
    gate_values,
    expert_gate_up,
    expert_down,
):
    token_count = queries.shape[0]
    req_count = lax.axis_size("req")
    wide_count = lax.axis_size("wide")
    segment, prefix = request_tables(suffix_lengths[0], prefix_ids[0], token_count)
    query_nope, query_rope = split_queries(queries)
    block_rows = prefix_latent.shape[2]
    key_owner = jnp.repeat(jnp.arange(PREF, dtype=jnp.int32), block_rows)
    group_prefix = lax.all_gather(prefix, "wide", axis=0, tiled=True)
    prefix_keys, prefix_values = split_kv(prefix_latent[0].reshape(PREF * block_rows, LAT), w_ukv)
    rope_keys = prefix_rope[0].transpose(1, 0, 2).reshape(ROPE, PREF * block_rows)
    piece_allowed = group_prefix[:, None] == key_owner[None, :]
    piece_nope, piece_rope = split_queries(lax.all_gather(queries, "wide", axis=0, tiled=True))
    remote_out, remote_max, remote_sum = block_partials(
        piece_nope, piece_rope, prefix_keys, prefix_values, rope_keys, piece_allowed
    )
    remote_out, remote_max, remote_sum = (
        lax.all_to_all(remote_out, "wide", split_axis=1, concat_axis=1, tiled=True),
        lax.all_to_all(remote_max, "wide", split_axis=1, concat_axis=1, tiled=True),
        lax.all_to_all(remote_sum, "wide", split_axis=1, concat_axis=1, tiled=True),
    )
    far_max = remote_max.astype(jnp.float32).reshape(HEADS, wide_count, token_count)
    far_sum = remote_sum.astype(jnp.float32).reshape(HEADS, wide_count, token_count)
    far_out = remote_out.reshape(HEADS, wide_count, token_count, NOPE)
    suffix_keys, suffix_values = split_kv(suffix_latent, w_ukv)
    positions = jnp.arange(token_count, dtype=jnp.int32)
    causal = (segment[:, None] == segment[None, :]) & (positions[None, :] <= positions[:, None])

    def local_head(operands):
        head_nope, head_rope, head_keys, head_values = operands
        scores = jnp.where(
            causal, head_scores(head_nope, head_rope, head_keys, suffix_rope), -jnp.inf
        )
        maximum = jnp.max(scores, axis=1)
        weights = jnp.where(causal, jnp.exp(scores - maximum[:, None]), 0.0)
        weighted = jnp.dot(
            weights.astype(jnp.bfloat16), head_values, preferred_element_type=jnp.float32
        )
        return (weighted, maximum, jnp.sum(weights, axis=1))

    local_out, local_max, local_sum = lax.map(
        local_head, (query_nope, query_rope, suffix_keys, suffix_values)
    )
    largest = jnp.maximum(local_max, jnp.max(far_max, axis=1))
    far_weight = jnp.exp(far_max - largest[:, None, :])
    near_weight = jnp.exp(local_max - largest)
    numerator = near_weight[:, :, None] * local_out + jnp.sum(
        far_weight[:, :, :, None] * far_out.astype(jnp.float32), axis=1
    )
    denominator = near_weight * local_sum + jnp.sum(far_weight * far_sum, axis=1)
    head_out = (numerator / denominator[:, :, None]).astype(jnp.bfloat16)
    attention = jnp.einsum(
        "htn,hnd->td", head_out, w_out.reshape(HEADS, NOPE, D), preferred_element_type=jnp.float32
    )
    hidden = (residual.astype(jnp.float32) + attention).astype(jnp.bfloat16)
    hidden_f32 = hidden.astype(jnp.float32)
    inverse = lax.rsqrt(jnp.mean(hidden_f32 * hidden_f32, axis=1, keepdims=True) + epsilon)
    normed = (hidden_f32 * inverse * norm_gain.astype(jnp.float32)[None, :]).astype(jnp.bfloat16)
    experts = req_count * wide_count // 2
    capacity = token_count * TOP // experts + 1
    flat_ids = expert_ids.reshape(-1)
    one_hot = (flat_ids[:, None] == jnp.arange(experts, dtype=jnp.int32)[None, :]).astype(jnp.int32)
    slot_index = jnp.sum((jnp.cumsum(one_hot, axis=0) - 1) * one_hot, axis=1)
    target = flat_ids * capacity + slot_index
    placement = jnp.arange(experts * capacity, dtype=jnp.int32)[:, None] == target[None, :]
    placed = placement.reshape(experts * capacity, token_count, TOP)
    dispatch_rows = jnp.any(placed, axis=2).astype(jnp.bfloat16)
    combine_rows = jnp.sum(jnp.where(placed, gate_values[None, :, :], 0.0), axis=2)
    outgoing = jnp.dot(dispatch_rows, normed, preferred_element_type=jnp.float32).astype(
        jnp.bfloat16
    )
    outgoing = outgoing.reshape(experts, capacity, D)
    doubled = jnp.broadcast_to(
        outgoing.reshape(experts, 1, capacity, D), (experts, 2, capacity, D)
    ).reshape(2 * experts, capacity, D)
    batch_in = lax.all_to_all(doubled, ("req", "wide"), split_axis=0, concat_axis=0, tiled=True)
    batch_shape = batch_in.shape
    flat_rows = batch_in.reshape(-1, D)
    gate_up = jnp.dot(flat_rows, expert_gate_up[0], preferred_element_type=jnp.float32)
    half_width = gate_up.shape[1] // 2
    activated = (jax.nn.silu(gate_up[:, :half_width]) * gate_up[:, half_width:]).astype(
        jnp.bfloat16
    )
    produced = jnp.dot(activated, expert_down[0], preferred_element_type=jnp.float32).astype(
        jnp.bfloat16
    )
    returned = lax.all_to_all(
        produced.reshape(batch_shape), ("req", "wide"), split_axis=0, concat_axis=0, tiled=True
    )
    halves = returned.reshape(experts, 2, capacity, D).astype(jnp.float32)
    summed_rows = (halves[:, 0] + halves[:, 1]).reshape(experts * capacity, D)
    mixture = lax.dot_general(
        combine_rows,
        summed_rows,
        (((0,), (0,)), ((), ())),
        precision=lax.Precision.HIGHEST,
        preferred_element_type=jnp.float32,
    )
    return (hidden_f32 + mixture).astype(jnp.bfloat16)


def solution(mesh):
    return jax.shard_map(
        body,
        mesh=mesh,
        in_specs=(
            P(("req", "wide"), None),
            P(("req", "wide"), None),
            P(None, ("req", "wide")),
            P(("req", "wide"), None),
            P("req", None, "wide", None),
            P("req", None, None, "wide"),
            P(("req", "wide"), None),
            P(("req", "wide"), None),
            P(),
            P(),
            P(),
            P(("req", "wide"), None),
            P(("req", "wide"), None),
            P(("req", "wide"), None, None),
            P(("req", "wide"), None, None),
        ),
        out_specs=P(("req", "wide"), None),
        check_vma=False,
    )
```

profile of v0, /device:TPU:37, one launch (start us, length us, event | category | flops | bytes accessed | tf_op | source)
XLA Modules:
  0.0 731.8 jit_solution(18404223918668810969)
XLA Ops:
  22.1 17.1 %all-gather = s32[16,1,128]{2,1,0:T(1,128)S(1)} all-gather(s32[1,1,128]{2,1,0:T(1,128)S(1)} %bitcast.195), channel_id=1, replica_groups=mesh['req'=8,'wide'=16] {'wide'}, dimensions={0}, use_global_device_ids=true | all-gather | bytes 8704 | tf_op jit(solution)/shard_map/all_gather | solution.py:90
  44.7 62.2 %all-gather.3.cloned.1.call-done = bf16[2048,3072]{0,1:T(8,128)(2,1)} async-done(((bf16[128,3072]{0,1:T(8,128)(2,1)}), bf16[2048,3072]{0,1:T(8,128)(2,1)}) %all-gather.3.cloned.1.call-update) | async-done | bytes 12582928 | tf_op jit(solution)/shard_map/all_gather | solution.py:94
  106.9 8.2 %slice.60 = bf16[2048,2048]{0,1:T(8,128)(2,1)} slice(bf16[2048,3072]{0,1:T(8,128)(2,1)} %all-gather.3.cloned.1.call-done), slice={[0:2048], [0:2048]} | slice | bytes 16777216 | tf_op jit(solution)/shard_map/slice | solution.py:34
  119.9 98.8 %while.31 = (s32[]{:T(128)}, bf16[16,2048,128]{2,1,0:T(8,128)(2,1)}, bf16[16,2048]{1,0:T(8,128)(2,1)S(1)}, bf16[16,2048]{1,0:T(8,128)(2,1)S(1)}, bf16[16,2048,12...) while((s32[]{:T(128)}, ...), condition=%wide.region_10.11_spmd.clone, body=%wide.region_7.10_spmd.clone.sunk | while | flops 342620160 | bytes 12060293 | solution.py:63
  219.4 6.4 all-to-all-start
  230.3 5.4 all-to-all-start.2
  240.1 10.3 %copy.147 = bf16[16,2048,128]{2,0,1:T(8,128)(2,1)} copy(bf16[16,2048,128]{2,1,0:T(8,128)(2,1)} %get-tuple-element.116) | data formatting | bytes 16777216 | tf_op jit(solution)/shard_map/while | solution.py:63
  251.1 6.7 all-to-all-start.1
  257.7 136.6 %while.30 = (s32[]{:T(128)}, f32[16,128,128]{2,0,1:T(8,128)}, f32[16,128]{1,0:T(8,128)}, f32[16,128]{1,0:T(8,128)}, bf16[16,128,128]{1,2,0:T(8,128)(2,1)S(1)}, /...) while((s32[]{:T(128)}, f32[16,128,128]{2,0,1:T(8,128)}, ...), condition=%wide.region_5.6_spmd.clone, body=%wide.region_2.5_spmd.clone.sunk | while | flops 10796802 | bytes 664193 | solution.py:122
  399.1 6.6 fusion.52
  406.5 4.8 multiply_reduce_fusion
  415.3 5.0 broadcast_in_dim.103
  420.3 6.8 broadcast_in_dim.104
  427.0 107.6 %all_to_all.33 = bf16[128,13,2048]{2,1,0:T(8,128)(2,1)} all-to-all(bf16[128,13,2048]{2,1,0:T(8,128)(2,1)} %bitcast.180), channel_id=1, replica_groups=mesh['req'=8,'wide'=16] {'req','wide'}, dimensions={0} | all-to-all | bytes 13631488 | tf_op jit(solution)/shard_map/all_to_all | solution.py:157
  534.6 9.3 %reshape.162 = bf16[1664,2048]{1,0:T(8,128)(2,1)} reshape(bf16[128,13,2048]{2,1,0:T(8,128)(2,1)} %all_to_all.33) | data formatting | bytes 13631488 | tf_op jit(solution)/shard_map/reshape | solution.py:159
  543.9 15.1 %fusion.54 = f32[1664,1408]{0,1:T(8,128)S(1)} fusion(bf16[1664,2048]{1,0:T(8,128)(2,1)} %reshape.162, bf16[1,2048,1408]{2,1,0:T(8,128)(2,1)} %param.32), kind=kOutput, calls=%fused_computation.60 | convolution fusion | flops 9596567552 | bytes 21954560 | tf_op jit(solution)/shard_map/dot_general | solution.py:160
  559.0 7.8 %convolution_convert_fusion.1 = bf16[1664,2048]{1,0:T(8,128)(2,1)} fusion(bf16[1,704,2048]{2,1,0:T(8,128)(2,1)S(1)} %copy-done, f32[1664,1408]{0,1:T(8,128)S(1)} %fusion.54), kind=kOutput, calls=%fused_computation.59 | convolution fusion | flops 4808720384 | bytes 19070976 | tf_op jit(solution)/shard_map/dot_general | solution.py:165
  566.8 9.1 %reshape.163 = bf16[128,13,2048]{2,1,0:T(8,128)(2,1)} reshape(bf16[1664,2048]{1,0:T(8,128)(2,1)} %convolution_convert_fusion.1) | data formatting | bytes 13631488 | tf_op jit(solution)/shard_map/reshape | solution.py:169
  575.9 8.5 %all-to-all-start.4 = ((bf16[128,13,2048]{2,1,0:T(8,128)(2,1)}), bf16[128,13,2048]{2,1,0:T(8,128)(2,1)}, u32[]{:S(2)}, u32[]{:S(2)}) async-start(bf16[128,13,2048]{2,1,0:T(8,128)(2,1)} %reshape.163), calls=%async_computation.4 | async-start | bytes 16777216 | tf_op jit(solution)/shard_map/all_to_all | solution.py:168
  584.7 103.2 %all-to-all-done.4 = bf16[128,13,2048]{2,1,0:T(8,128)(2,1)} async-done(((bf16[128,13,2048]{2,1,0:T(8,128)(2,1)}), bf16[128,13,2048]{2,1,0:T(8,128)(2,1)}, u32[]{:S(2)}, u32[]{:S(2)}) %all-to-all-start.4) | async-done | bytes 6815776 | tf_op jit(solution)/shard_map/all_to_all | solution.py:168
  687.9 11.2 %convert.4 = f32[64,2,13,2048]{3,2,1,0:T(8,128)} convert(bf16[64,2,13,2048]{3,2,1,0:T(8,128)(2,1)} %bitcast.27) | non-fusion elementwise | flops 3407872 | bytes 20447232 | tf_op jit(solution)/shard_map/convert_element_type | solution.py:171
  699.2 11.7 %fusion.53 = f32[64,1,13,2048]{3,2,0,1:T(8,128)} fusion(f32[64,2,13,2048]{3,2,1,0:T(8,128)} %convert.4), kind=kLoop, calls=%fused_computation.57 | loop fusion | flops 1703936 | bytes 20447232 | tf_op jit(solution)/shard_map/add | solution.py:172
  710.9 6.8 add.64
  717.6 7.3 fusion.62
  (338 shorter events, 280.1 us)
Async XLA Ops:
  6.5 552.4 %copy-start = (bf16[1,704,2048]{2,1,0:T(8,128)(2,1)S(1)}, bf16[1,704,2048]{2,1,0:T(8,128)(2,1)}, u32[]{:S(2)}) copy-start(bf16[1,704,2048]{2,1,0:T(8,128)(2,1)} %param.33) | copy-start | bytes 8650756
  6.5 100.4 %all-gather.3.cloned.1.call-start = ((), (), s32[]{:S(2)}) async-start(), calls=%async_computation.5 | async-start | bytes 13369344 | tf_op jit(solution)/shard_map/all_gather | solution.py:94
  13.7 1.6 copy-start.13
  13.7 1.8 copy-start.7
  15.4 6.6 copy-start.14
  15.4 23.9 %copy-start.10 = (s32[128,6]{0,1:T(8,128)S(1)}, s32[128,6]{0,1:T(8,128)}, u32[]{:S(2)}) copy-start(s32[128,6]{0,1:T(8,128)} %param.30) | copy-start | bytes 9220
  15.4 23.9 %copy-start.9 = (bf16[1,2,64,128]{3,2,1,0:T(8,128)(2,1)S(1)}, bf16[1,2,64,128]{3,2,1,0:T(8,128)(2,1)}, u32[]{:S(2)}) copy-start(bf16[1,2,64,128]{3,2,1,0:T(8,128)(2,1)} %param.24) | copy-start | bytes 98308
  119.9 119.6 %copy-start.12 = (bf16[2048]{0:T(1024)(128)(2,1)S(1)}, bf16[2048]{0:T(1024)(128)(2,1)}, u32[]{:S(2)}) copy-start(bf16[2048]{0:T(1024)(128)(2,1)} %param.29) | copy-start | bytes 12292
  219.4 10.9 %all-to-all-start = ((bf16[16,16,128]{2,0,1:T(8,128)(2,1)}), bf16[16,16,128]{2,0,1:T(8,128)(2,1)S(1)}, u32[]{:S(2)}, u32[]{:S(2)}) async-start(bf16[16,16,128]{2,0,1:T(8,128)(2,1)} %copy_bitcast_fusion.1), calls=%async_computation | async-start | bytes 131072 | tf_op jit(solution)/shard_map/all_to_all | solution.py:100
  230.3 20.1 %copy-start.4 = (bf16[16,16,128]{2,0,1:T(8,128)(2,1)}, bf16[16,16,128]{2,0,1:T(8,128)(2,1)S(1)}, u32[]{:S(2)}) copy-start(bf16[16,16,128]{2,0,1:T(8,128)(2,1)S(1)} %all-to-all-done) | copy-start | bytes 196612
  230.3 20.1 %all-to-all-start.2 = ((bf16[16,16,128]{2,0,1:T(8,128)(2,1)}), bf16[16,16,128]{2,0,1:T(8,128)(2,1)S(1)}, u32[]{:S(2)}, u32[]{:S(2)}) async-start(bf16[16,16,128]{2,0,1:T(8,128)(2,1)} %copy_bitcast_fusion), calls=%async_computation.2 | async-start | bytes 131072 | tf_op jit(solution)/shard_map/all_to_all | solution.py:101
  250.4 0.6 copy-start.6
  251.1 148.1 %all-to-all-start.1 = ((bf16[16,2048,128]{2,0,1:T(8,128)(2,1)}), bf16[16,2048,128]{2,0,1:T(8,128)(2,1)}, u32[]{:S(2)}, u32[]{:S(2)}) async-start(bf16[16,2048,128]{2,0,1:T(8,128)(2,1)} %copy.147), calls=%async_computation.1 | async-start | bytes 16777216 | tf_op jit(solution)/shard_map/all_to_all | solution.py:99
  399.1 6.6 copy-start.2
  399.1 7.3 %copy-start.5 = (bf16[128,2048]{1,0:T(8,128)(2,1)S(1)}, bf16[128,2048]{1,0:T(8,128)(2,1)}, u32[]{:S(2)}) copy-start(bf16[128,2048]{1,0:T(8,128)(2,1)} %param.22) | copy-start | bytes 1572868
  406.5 5.9 copy-start.3
  406.5 5.9 copy-start.8
  411.4 1.1 copy-start.1
  575.8 8.5 %copy-start.11 = (f32[128,6]{0,1:T(8,128)S(1)}, f32[128,6]{0,1:T(8,128)}, u32[]{:S(2)}) copy-start(f32[128,6]{0,1:T(8,128)} %param.31) | copy-start | bytes 9220
  575.9 112.1 %all-to-all-start.4 = ((bf16[128,13,2048]{2,1,0:T(8,128)(2,1)}), bf16[128,13,2048]{2,1,0:T(8,128)(2,1)}, u32[]{:S(2)}, u32[]{:S(2)}) async-start(bf16[128,13,2048]{2,1,0:T(8,128)(2,1)} %reshape.163), calls=%async_computation.4 | async-start | bytes 16777216 | tf_op jit(solution)/shard_map/all_to_all | solution.py:168
Sparse Core Ops, SparseCore 0:
  9.4 97.4 all-gather.2
where the time goes:
time: 739 us; the launch traced here: 732 us
  matrix products  177 us (24%)
  local copies, waits for them, and re-layouts  172 us (23%)
  waiting for transfers between devices  169 us (23%)
  blocking collectives  125 us (17%)
  other arithmetic  46.8 us (6%)
  starting transfers between devices  26.9 us (4%)
  between operations  13.7 us (2%)
    all_to_all x1, blocking collectives, body(): lax.all_to_all(doubled, ('req', 'wide'), split_axis=0, concat_axis=0, til...  108 us
    all_to_all x1, waiting for transfers between devices, body(): lax.all_to_all(produced.reshape(batch_shape), ('req', 'wide'), split_axis...  103 us
    dynamic_update_slice x48, local copies, waits for them, and re-layouts, body(): lax.map(local_head, (query_nope, query_rope, suffix_keys, suffix_values))  88.7 us
    all_gather x1, waiting for transfers between devices, body(): lax.all_gather(queries, 'wide', axis=0, tiled=True)  62.2 us
    dot_general x32, matrix products, head_scores(): rotary = jnp.dot(head_rope, rope_keys, preferred_element_type=jnp.float32)  39.9 us
    dot_general x32, matrix products, head_scores(): lax.dot_general(head_nope, head_keys, (((1,), (1,)), ((), ())), preferred...  38.9 us
    dot_general x16, matrix products, one_head(): jnp.dot(weights.astype(jnp.bfloat16), head_values, preferred_element_type...  37.5 us
    all_gather x1, blocking collectives, body(): group_prefix = lax.all_gather(prefix, 'wide', axis=0, tiled=True)  17.1 us
  transfers between devices with their start and end apart: 5, of which 3 were waited for; matrix products, arithmetic and copies ran while one was open for 24% of the time, Pallas kernels for 0%

commit v1 on v0

--- a/solution.py
+++ b/solution.py
@@ -11,6 +11,11 @@
 TOP = 6
 PREF = 2
 epsilon = 1e-06
+
+
+def swapped_in(array, mesh_axis, along):
+    sent = jnp.stack([array] * lax.axis_size(mesh_axis))
+    return jnp.concatenate(lax.all_to_all(sent, mesh_axis, 0, 0), axis=along)
 
 
 def request_tables(lengths, request_ids, token_count):
@@ -91,7 +96,7 @@
     prefix_keys, prefix_values = split_kv(prefix_latent[0].reshape(PREF * block_rows, LAT), w_ukv)
     rope_keys = prefix_rope[0].transpose(1, 0, 2).reshape(ROPE, PREF * block_rows)
     piece_allowed = group_prefix[:, None] == key_owner[None, :]
-    piece_nope, piece_rope = split_queries(lax.all_gather(queries, "wide", axis=0, tiled=True))
+    piece_nope, piece_rope = split_queries(swapped_in(queries, "wide", 0))
     remote_out, remote_max, remote_sum = block_partials(
         piece_nope, piece_rope, prefix_keys, prefix_values, rope_keys, piece_allowed
     )

time: 739 us -> 891 us (1.21)
  blocking collectives: 125 us -> 328 us
  waiting for transfers between devices: 169 us -> 107 us
  local copies, waits for them, and re-layouts: 172 us -> 189 us
  between operations: 13.7 us -> 0.26 us
    all_gather x1, blocking collectives: 17.1 us -> 216 us  [body(): group_prefix = lax.all_gather(prefix, 'wide', axis=0, tiled=True)]
    all_gather x1 -> x0, waiting for transfers between devices: 62.2 us -> none  [body(): lax.all_gather(queries, 'wide', axis=0, tiled=True)]
    reshape x0 -> x1, local copies, waits for them, and re-layouts: none -> 10.9 us  [swapped_in(): return jnp.concatenate(lax.all_to_all(sent, mesh_axis, 0, 0), axis=along)]
  transfers between devices with their start and end apart: 5 -> 5, of which waited for: 3 -> 2; matrix products, arithmetic and copies ran while one was open for 24% -> 20% of each run, Pallas kernels for 0% -> 0%
where the time goes in v1:
time: 891 us; the launch traced here: 883 us
  blocking collectives  328 us (37%)
  local copies, waits for them, and re-layouts  189 us (21%)
  matrix products  177 us (20%)
  waiting for transfers between devices  107 us (12%)
  other arithmetic  46.8 us (5%)
  starting transfers between devices  34 us (4%)
    all_gather x1, blocking collectives, body(): group_prefix = lax.all_gather(prefix, 'wide', axis=0, tiled=True)  216 us
    all_to_all x1, blocking collectives, body(): lax.all_to_all(doubled, ('req', 'wide'), split_axis=0, concat_axis=0, til...  111 us
    all_to_all x1, waiting for transfers between devices, body(): lax.all_to_all(produced.reshape(batch_shape), ('req', 'wide'), split_axis...  103 us
    dynamic_update_slice x48, local copies, waits for them, and re-layouts, body(): lax.map(local_head, (query_nope, query_rope, suffix_keys, suffix_values))  88.6 us
    dot_general x32, matrix products, head_scores(): rotary = jnp.dot(head_rope, rope_keys, preferred_element_type=jnp.float32)  39.9 us
    dot_general x32, matrix products, head_scores(): lax.dot_general(head_nope, head_keys, (((1,), (1,)), ((), ())), preferred...  38.9 us
    dot_general x16, matrix products, one_head(): jnp.dot(weights.astype(jnp.bfloat16), head_values, preferred_element_type...  37.5 us
  transfers between devices with their start and end apart: 5, of which 2 were waited for; matrix products, arithmetic and copies ran while one was open for 20% of the time, Pallas kernels for 0%

profile of v1, /device:TPU:37, one launch (start us, length us, event | category | flops | bytes accessed | tf_op | source)
XLA Modules:
  0.0 883.3 jit_solution(5328446779660520221)
XLA Ops:
  2.5 8.0 stack.2
  10.5 7.0 all-to-all-start
  29.9 216.2 %all-gather = s32[16,1,128]{2,1,0:T(1,128)S(1)} all-gather(s32[1,1,128]{2,1,0:T(1,128)S(1)} %bitcast.200), channel_id=1, replica_groups=mesh['req'=8,'wide'=16] {'wide'}, dimensions={0}, use_global_device_ids=true | all-gather | bytes 8704 | tf_op jit(solution)/shard_map/all_gather | solution.py:95
  251.6 10.9 %copy_bitcast_fusion = bf16[2048,3072]{0,1:T(8,128)(2,1)} fusion(bf16[16,128,3072]{1,2,0:T(8,128)(2,1)} %all-to-all-done), kind=kLoop, calls=%fused_computation.56 | loop fusion | bytes 25165824 | tf_op jit(solution)/shard_map/reshape | solution.py:18
  262.4 8.3 slice.60
  275.4 98.8 %while.31 = (s32[]{:T(128)}, bf16[16,2048,128]{2,1,0:T(8,128)(2,1)}, bf16[16,2048]{1,0:T(8,128)(2,1)S(1)}, bf16[16,2048]{1,0:T(8,128)(2,1)S(1)}, bf16[16,2048,12...) while((s32[]{:T(128)}, ...), condition=%wide.region_10.11_spmd.clone, body=%wide.region_7.10_spmd.clone.sunk | while | flops 342620160 | bytes 12060293 | solution.py:68
  374.9 6.4 all-to-all-start.1
  385.9 5.4 all-to-all-start.3
  394.6 10.3 %copy.152 = bf16[16,2048,128]{2,0,1:T(8,128)(2,1)} copy(bf16[16,2048,128]{2,1,0:T(8,128)(2,1)} %get-tuple-element.116) | data formatting | bytes 16777216 | tf_op jit(solution)/shard_map/while | solution.py:68
  405.6 6.7 all-to-all-start.2
  412.3 136.5 %while.30 = (s32[]{:T(128)}, f32[16,128,128]{2,0,1:T(8,128)}, f32[16,128]{1,0:T(8,128)}, f32[16,128]{1,0:T(8,128)}, bf16[16,128,128]{1,2,0:T(8,128)(2,1)S(1)}, /...) while((s32[]{:T(128)}, f32[16,128,128]{2,0,1:T(8,128)}, ...), condition=%wide.region_5.6_spmd.clone, body=%wide.region_2.5_spmd.clone.sunk | while | flops 10796802 | bytes 664193 | solution.py:127
  553.6 6.6 fusion.52
  574.7 6.8 broadcast_in_dim.104
  581.5 111.5 %all_to_all.38 = bf16[128,13,2048]{2,1,0:T(8,128)(2,1)} all-to-all(bf16[128,13,2048]{2,1,0:T(8,128)(2,1)} %bitcast.185), channel_id=1, replica_groups=mesh['req'=8,'wide'=16] {'req','wide'}, dimensions={0} | all-to-all | bytes 13631488 | tf_op jit(solution)/shard_map/all_to_all | solution.py:162
  692.9 9.3 %reshape.168 = bf16[1664,2048]{1,0:T(8,128)(2,1)} reshape(bf16[128,13,2048]{2,1,0:T(8,128)(2,1)} %all_to_all.38) | data formatting | bytes 13631488 | tf_op jit(solution)/shard_map/reshape | solution.py:164
  702.2 15.1 %fusion.54 = f32[1664,1408]{0,1:T(8,128)S(1)} fusion(bf16[1664,2048]{1,0:T(8,128)(2,1)} %reshape.168, bf16[1,2048,1408]{2,1,0:T(8,128)(2,1)} %param.32), kind=kOutput, calls=%fused_computation.61 | convolution fusion | flops 9596567552 | bytes 21954560 | tf_op jit(solution)/shard_map/dot_general | solution.py:165
  717.3 7.8 convolution_convert_fusion.1
  725.1 9.1 %reshape.169 = bf16[128,13,2048]{2,1,0:T(8,128)(2,1)} reshape(bf16[1664,2048]{1,0:T(8,128)(2,1)} %convolution_convert_fusion.1) | data formatting | bytes 13631488 | tf_op jit(solution)/shard_map/reshape | solution.py:174
  734.2 8.5 all-to-all-start.5
  743.0 103.2 %all-to-all-done.5 = bf16[128,13,2048]{2,1,0:T(8,128)(2,1)} async-done(((bf16[128,13,2048]{2,1,0:T(8,128)(2,1)}), bf16[128,13,2048]{2,1,0:T(8,128)(2,1)}, u32[]{:S(2)}, u32[]{:S(2)}) %all-to-all-start.5) | async-done | bytes 6815776 | tf_op jit(solution)/shard_map/all_to_all | solution.py:173
  846.3 11.2 %convert.4 = f32[64,2,13,2048]{3,2,1,0:T(8,128)} convert(bf16[64,2,13,2048]{3,2,1,0:T(8,128)(2,1)} %bitcast.27) | non-fusion elementwise | flops 3407872 | bytes 20447232 | tf_op jit(solution)/shard_map/convert_element_type | solution.py:176
  857.5 11.7 %fusion.53 = f32[64,1,13,2048]{3,2,0,1:T(8,128)} fusion(f32[64,2,13,2048]{3,2,1,0:T(8,128)} %convert.4), kind=kLoop, calls=%fused_computation.58 | loop fusion | flops 1703936 | bytes 20447232 | tf_op jit(solution)/shard_map/add | solution.py:177
  869.2 6.8 add.64
  876.0 7.3 fusion.62
  (340 shorter events, 288.1 us)
Async XLA Ops:
  0.0 717.3 %copy-start = (bf16[1,704,2048]{2,1,0:T(8,128)(2,1)S(1)}, bf16[1,704,2048]{2,1,0:T(8,128)(2,1)}, u32[]{:S(2)}) copy-start(bf16[1,704,2048]{2,1,0:T(8,128)(2,1)} %param.33) | copy-start | bytes 8650756
  10.5 7.1 copy-start.10
  10.5 241.1 %all-to-all-start = ((bf16[16,128,3072]{1,2,0:T(8,128)(2,1)}), bf16[16,128,3072]{1,2,0:T(8,128)(2,1)}, u32[]{:S(2)}, u32[]{:S(2)}) async-start(bf16[16,128,3072]{1,2,0:T(8,128)(2,1)} %stack.2), calls=%async_computation | async-start | bytes 25165824 | tf_op jit(solution)/shard_map/all_to_all | solution.py:18
  17.9 5.1 copy-start.13
  17.9 5.3 copy-start.7
  23.1 6.7 copy-start.14
  23.1 223.0 %copy-start.9 = (bf16[1,2,64,128]{3,2,1,0:T(8,128)(2,1)S(1)}, bf16[1,2,64,128]{3,2,1,0:T(8,128)(2,1)}, u32[]{:S(2)}) copy-start(bf16[1,2,64,128]{3,2,1,0:T(8,128)(2,1)} %param.24) | copy-start | bytes 98308
  275.4 118.5 %copy-start.12 = (bf16[2048]{0:T(1024)(128)(2,1)S(1)}, bf16[2048]{0:T(1024)(128)(2,1)}, u32[]{:S(2)}) copy-start(bf16[2048]{0:T(1024)(128)(2,1)} %param.29) | copy-start | bytes 12292
  374.9 11.0 %all-to-all-start.1 = ((bf16[16,16,128]{2,0,1:T(8,128)(2,1)}), bf16[16,16,128]{2,0,1:T(8,128)(2,1)S(1)}, u32[]{:S(2)}, u32[]{:S(2)}) async-start(bf16[16,16,128]{2,0,1:T(8,128)(2,1)} %copy_bitcast_fusion.2), calls=%async_computation.1 | async-start | bytes 131072 | tf_op jit(solution)/shard_map/all_to_all | solution.py:105
  385.9 19.0 %copy-start.4 = (bf16[16,16,128]{2,0,1:T(8,128)(2,1)}, bf16[16,16,128]{2,0,1:T(8,128)(2,1)S(1)}, u32[]{:S(2)}) copy-start(bf16[16,16,128]{2,0,1:T(8,128)(2,1)S(1)} %all-to-all-done.1) | copy-start | bytes 196612
  385.9 19.0 %all-to-all-start.3 = ((bf16[16,16,128]{2,0,1:T(8,128)(2,1)}), bf16[16,16,128]{2,0,1:T(8,128)(2,1)S(1)}, u32[]{:S(2)}, u32[]{:S(2)}) async-start(bf16[16,16,128]{2,0,1:T(8,128)(2,1)} %copy_bitcast_fusion.1), calls=%async_computation.3 | async-start | bytes 131072 | tf_op jit(solution)/shard_map/all_to_all | solution.py:106
  404.9 7.3 slice-start
  404.9 0.6 copy-start.6
  405.6 148.0 %all-to-all-start.2 = ((bf16[16,2048,128]{2,0,1:T(8,128)(2,1)}), bf16[16,2048,128]{2,0,1:T(8,128)(2,1)}, u32[]{:S(2)}, u32[]{:S(2)}) async-start(bf16[16,2048,128]{2,0,1:T(8,128)(2,1)} %copy.152), calls=%async_computation.2 | async-start | bytes 16777216 | tf_op jit(solution)/shard_map/all_to_all | solution.py:104
  553.6 6.6 copy-start.2
  553.6 7.3 copy-start.5
  560.9 5.9 copy-start.3
  560.9 5.9 copy-start.8
  565.8 1.1 copy-start.1
  734.2 8.5 copy-start.11
  734.2 112.1 %all-to-all-start.5 = ((bf16[128,13,2048]{2,1,0:T(8,128)(2,1)}), bf16[128,13,2048]{2,1,0:T(8,128)(2,1)}, u32[]{:S(2)}, u32[]{:S(2)}) async-start(bf16[128,13,2048]{2,1,0:T(8,128)(2,1)} %reshape.169), calls=%async_computation.5 | async-start | bytes 16777216 | tf_op jit(solution)/shard_map/all_to_all | solution.py:173
